TPU v7x, 32 devices: a whole 2x2x4 slice. The times are simulated.
32 devices in a mesh: rep: 2 (over core), shard: 16 (over z, y, x).
Axes of the slice: x: 2, y: 2, z: 4, core: 2. Of those that a mesh axis runs over, the one named last changes fastest.
Arguments:
- tokens: bfloat16 [32, 1024, 768], P('rep', 'shard'), may hold values from -6 to 6
- cotangent: bfloat16 [32, 1024, 768], P('rep', 'shard'), may hold values from -6 to 6
- lengths: int32 [2, 16], P('rep'), may hold values from 512 to 1024, as said below
- order: int32 [2, 16], P('rep'), may hold values from 0 to 15, each once within a row
- norm_weight: bfloat16 [768], P('shard'), may hold values from 0.099609375 to 1.8984375
- in_weight: bfloat16 [768, 3352], P('shard'), may hold values from -0.21875 to 0.21875
- conv_weight: bfloat16 [1792, 4], P('shard'), may hold values from -3 to 3
- conv_bias: bfloat16 [1792], P('shard'), may hold values from -3 to 3
- step_bias: float32 [24], replicated, may hold values from -5.5 to -2.5
- decay_log: float32 [24], replicated, may hold values from 0 to 2.77
- skip_gain: float32 [24], replicated, may hold values from 0.5 to 1.5
- gate_norm_weight: bfloat16 [1536], P('shard'), may hold values from 0.099609375 to 1.8984375
- out_weight: bfloat16 [1536, 768], P('shard'), may hold values from -0.15625 to 0.15625
Outputs:
- output: bfloat16 [32, 1024, 768], P('rep', 'shard')
- input_grad: bfloat16 [32, 1024, 768], P('rep', 'shard')
- grad_norm: float32 [768], P('shard')
- grad_in: float32 [768, 3352], P('shard')
- grad_conv: float32 [1792, 4], P('shard')
- grad_conv_bias: float32 [1792], P('shard')
- grad_step_bias: float32 [24], replicated
- grad_decay_log: float32 [24], replicated
- grad_skip: float32 [24], replicated
- grad_gate_norm: float32 [1536], P('shard')
- grad_out: float32 [1536, 768], P('shard')
Inputs may be any that keep to these rules, and one draw needn't show every extreme that they name: Each row of order holds every number from 0 to 15 once: slot k of group r holds sequence order[r, k]. lengths[r, s] counts the valid leading positions of sequence s of group r; each row has one entry equal to 1024 and one equal to 512.
All inputs are finite; a program needn't handle non-finite values.
Results may differ from a plain program's by a relative error of at most 0.012.
The roundings to bfloat16 on the way count: a program that leaves them out, or rounds other values in their place, can miss the bound.
Values may be sent and summed in bfloat16 or wider, within the bound.
A program may use at most 192 MiB of HBM per device.

v0:
```python
import jax
import jax.numpy as jnp
from jax import lax
from jax.sharding import PartitionSpec as P

HEADS = 24
HEADDIM = 64
STATE = 128
CONV = 4
SPAN = 256
DI = 1536
XBC = 1792
epsilon = 1e-05


def decay_terms(log_block, step_block):
    cumul = jnp.cumsum(log_block, axis=0)
    cumul_heads = cumul.T
    positions = log_block.shape[0]
    causal = jnp.arange(positions)[:, None] >= jnp.arange(positions)[None, :]
    spread = jnp.where(causal[None], cumul_heads[:, :, None] - cumul_heads[:, None, :], 0.0)
    factor = jnp.where(causal[None], jnp.exp(spread), 0.0) * step_block.T[:, None, :]
    carry_weight = jnp.exp(cumul[-1][None, :] - cumul) * step_block
    return (factor, carry_weight, jnp.exp(cumul), jnp.exp(cumul[-1]))


def norm_part(tok_float, norm_gain):
    return (
        tok_float
        * lax.rsqrt(jnp.mean(tok_float * tok_float, axis=-1, keepdims=True) + epsilon)
        * norm_gain
    )


def conv_part(conv_in, conv_taps, conv_shift):
    length = conv_in.shape[0]
    padded = jnp.concatenate(
        [jnp.zeros((CONV - 1, conv_in.shape[1]), jnp.float32), conv_in], axis=0
    )
    total = conv_shift[None, :] + jnp.zeros_like(conv_in)
    for tap in range(CONV):
        total = total + conv_taps[:, tap][None, :] * padded[tap : tap + length]
    return jax.nn.silu(total)


def step_part(step_raw, step_bias, decay_log):
    step_size = jax.nn.softplus(step_raw + step_bias[None, :])
    return (step_size, -jnp.exp(decay_log)[None, :] * step_size)


def gate_part(scan_out, heads_in, skip_gain, gate_raw, gate_gain):
    mixed = scan_out + jnp.repeat(skip_gain, HEADDIM)[None, :] * heads_in
    gated = mixed * jax.nn.silu(gate_raw)
    return gated * lax.rsqrt(jnp.mean(gated * gated, axis=-1, keepdims=True) + epsilon) * gate_gain


def block_forward(state, inputs):
    heads_blk, keys_blk, query_blk, step_blk, log_blk = inputs
    factor, carry_weight, growth, growth_last = decay_terms(log_blk, step_blk)
    scores = jnp.einsum("tn,sn->ts", query_blk, keys_blk, preferred_element_type=jnp.float32)
    mixing = (scores[None] * factor).astype(jnp.bfloat16)
    within = jnp.einsum("hts,shp->thp", mixing, heads_blk, preferred_element_type=jnp.float32)
    across = jnp.einsum(
        "tn,hpn->thp", query_blk, state.astype(jnp.bfloat16), preferred_element_type=jnp.float32
    )
    result = within + growth[:, :, None] * across
    weighted = (heads_blk.astype(jnp.float32) * carry_weight[:, :, None]).astype(jnp.bfloat16)
    contrib = jnp.einsum("sn,shp->hpn", keys_blk, weighted, preferred_element_type=jnp.float32)
    return (growth_last[:, None, None] * state + contrib, (result, state))


def block_backward(later, inputs):
    heads_blk, keys_blk, query_blk, step_blk, log_blk, grad_blk, state = inputs
    terms, decay_pull = jax.vjp(decay_terms, log_blk, step_blk)
    factor, carry_weight, growth, growth_last = terms
    scores = jnp.einsum("tn,sn->ts", query_blk, keys_blk, preferred_element_type=jnp.float32)
    mixing = (scores[None] * factor).astype(jnp.bfloat16)
    state_low = state.astype(jnp.bfloat16)
    across = jnp.einsum("tn,hpn->thp", query_blk, state_low, preferred_element_type=jnp.float32)
    heads_float = heads_blk.astype(jnp.float32)
    weighted = (heads_float * carry_weight[:, :, None]).astype(jnp.bfloat16)
    grad_within = grad_blk.astype(jnp.bfloat16)
    grad_across = (growth[:, :, None] * grad_blk).astype(jnp.bfloat16)
    grad_mixing = jnp.einsum(
        "thp,shp->hts", grad_within, heads_blk, preferred_element_type=jnp.float32
    )
    grad_heads = jnp.einsum("hts,thp->shp", mixing, grad_within, preferred_element_type=jnp.float32)
    grad_query = jnp.einsum(
        "thp,hpn->tn", grad_across, state_low, preferred_element_type=jnp.float32
    )
    grad_state = jnp.einsum(
        "thp,tn->hpn", grad_across, query_blk, preferred_element_type=jnp.float32
    )
    grad_state = grad_state + growth_last[:, None, None] * later
    grad_growth = jnp.sum(grad_blk * across, axis=2)
    later_low = later.astype(jnp.bfloat16)
    grad_weighted = jnp.einsum(
        "hpn,sn->shp", later_low, keys_blk, preferred_element_type=jnp.float32
    )
    grad_keys = jnp.einsum("hpn,shp->sn", later_low, weighted, preferred_element_type=jnp.float32)
    grad_heads = grad_heads + grad_weighted * carry_weight[:, :, None]
    grad_carry = jnp.sum(grad_weighted * heads_float, axis=2)
    grad_last = jnp.sum(later * state, axis=(1, 2))
    grad_scores = jnp.sum(grad_mixing * factor, axis=0).astype(jnp.bfloat16)
    grad_query = grad_query + jnp.dot(grad_scores, keys_blk, preferred_element_type=jnp.float32)
    grad_keys = grad_keys + jnp.einsum(
        "ts,tn->sn", grad_scores, query_blk, preferred_element_type=jnp.float32
    )
    grad_log, grad_step = decay_pull(
        (grad_mixing * scores[None], grad_carry, grad_growth, grad_last)
    )
    return (grad_state, (grad_heads, grad_keys, grad_query, grad_step, grad_log))


def forward_seq(
    tok_float,
    keep,
    norm_full,
    in_full,
    conv_full,
    shift_full,
    gate_full,
    out_full,
    step_bias,
    decay_log,
    skip_gain,
):
    seq_len = tok_float.shape[0]
    normed, norm_pull = jax.vjp(norm_part, tok_float, norm_full.astype(jnp.float32))
    normed_low = normed.astype(jnp.bfloat16)
    projected = jnp.dot(normed_low, in_full, preferred_element_type=jnp.float32)
    gate_raw = projected[:, :DI]
    conv_in = projected[:, DI : DI + XBC]
    step_raw = projected[:, DI + XBC :]
    convolved, conv_pull = jax.vjp(
        conv_part, conv_in, conv_full.astype(jnp.float32), shift_full.astype(jnp.float32)
    )
    heads_in = convolved[:, :DI]
    heads_low = heads_in.astype(jnp.bfloat16)
    key_low = convolved[:, DI : DI + STATE].astype(jnp.bfloat16)
    query_low = convolved[:, DI + STATE :].astype(jnp.bfloat16)
    decays, step_pull = jax.vjp(step_part, step_raw, step_bias, decay_log)
    step_size, log_decay = decays
    count = seq_len // SPAN
    blocks = (
        heads_low.reshape(count, SPAN, HEADS, HEADDIM),
        key_low.reshape(count, SPAN, STATE),
        query_low.reshape(count, SPAN, STATE),
        step_size.reshape(count, SPAN, HEADS),
        log_decay.reshape(count, SPAN, HEADS),
    )
    start = jnp.zeros((HEADS, HEADDIM, STATE), jnp.float32)
    final_state, kept = lax.scan(block_forward, start, blocks)
    scan_blocks, states = kept
    scan_out = scan_blocks.reshape(seq_len, DI)
    gate_value, gate_pull = jax.vjp(
        gate_part, scan_out, heads_in, skip_gain, gate_raw, gate_full.astype(jnp.float32)
    )
    gate_low = gate_value.astype(jnp.bfloat16)
    branch = jnp.dot(gate_low, out_full, preferred_element_type=jnp.float32)
    result = (tok_float + keep[:, None] * branch).astype(jnp.bfloat16)
    saved = (keep, normed_low, norm_pull, conv_pull, step_pull, gate_pull, gate_low, blocks, states)
    return (result, saved)


def backward_seq(saved, cot_float, in_full, out_full):
    keep, normed_low, norm_pull, conv_pull, step_pull, gate_pull, gate_low, blocks, states = saved
    seq_len = cot_float.shape[0]
    count = seq_len // SPAN
    grad_branch = (keep[:, None] * cot_float).astype(jnp.bfloat16)
    grad_out_full = jnp.einsum(
        "ti,tj->ij", gate_low, grad_branch, preferred_element_type=jnp.float32
    )
    grad_gate = jnp.einsum("tj,ij->ti", grad_branch, out_full, preferred_element_type=jnp.float32)
    grad_scan, grad_heads_skip, grad_skip, grad_gate_raw, grad_gate_gain = gate_pull(grad_gate)
    grad_scan_blocks = grad_scan.reshape(count, SPAN, HEADS, HEADDIM)
    first_grad, grads = lax.scan(
        block_backward,
        jnp.zeros((HEADS, HEADDIM, STATE), jnp.float32),
        (blocks[0], blocks[1], blocks[2], blocks[3], blocks[4], grad_scan_blocks, states),
        reverse=True,
    )
    grad_heads, grad_keys, grad_query, grad_step, grad_log = grads
    grad_step_raw, grad_step_bias, grad_decay_log = step_pull(
        (grad_step.reshape(seq_len, HEADS), grad_log.reshape(seq_len, HEADS))
    )
    grad_convolved = jnp.concatenate(
        [
            grad_heads.reshape(seq_len, DI) + grad_heads_skip,
            grad_keys.reshape(seq_len, STATE),
            grad_query.reshape(seq_len, STATE),
        ],
        axis=1,
    )
    grad_conv_in, grad_taps, grad_shift = conv_pull(grad_convolved)
    grad_projected = jnp.concatenate([grad_gate_raw, grad_conv_in, grad_step_raw], axis=1).astype(
        jnp.bfloat16
    )
    grad_in_full = jnp.einsum(
        "ti,tj->ij", normed_low, grad_projected, preferred_element_type=jnp.float32
    )
    grad_normed = jnp.einsum(
        "tj,ij->ti", grad_projected, in_full, preferred_element_type=jnp.float32
    )
    grad_tok, grad_norm_gain = norm_pull(grad_normed)
    input_grad = (cot_float + grad_tok).astype(jnp.bfloat16)
    weight_grads = (
        grad_norm_gain,
        grad_in_full,
        grad_taps,
        grad_shift,
        grad_gate_gain,
        grad_out_full,
    )
    return (input_grad, weight_grads, (grad_step_bias, grad_decay_log, grad_skip))


def on_device(
    tokens,
    cotangent,
    lengths,
    order,
    norm_weight,
    in_weight,
    conv_weight,
    conv_bias,
    step_bias,
    decay_log,
    skip_gain,
    gate_norm_weight,
    out_weight,
):
    peers = lax.axis_size("shard")
    rank = lax.axis_index("shard")
    slots = jnp.arange(peers, dtype=jnp.int32)
    order_row = order[0]
    inverse = jnp.sum(jnp.where(order_row[None, :] == slots[:, None], slots[None, :], 0), axis=1)
    piece = tokens.shape[1]
    width = tokens.shape[2]
    sent_tokens = jnp.take(tokens, inverse, axis=0).reshape(peers, 1, piece, width)
    sent_cot = jnp.take(cotangent, inverse, axis=0).reshape(peers, 1, piece, width)
    got_tokens, got_cot = (
        lax.all_to_all(sent_tokens, "shard", split_axis=0, concat_axis=2, tiled=True),
        lax.all_to_all(sent_cot, "shard", split_axis=0, concat_axis=2, tiled=True),
    )
    seq_len = got_tokens.shape[2]
    length_row = lengths[0]
    gathered = (
        lax.all_gather(norm_weight, "shard", axis=0, tiled=True),
        lax.all_gather(in_weight, "shard", axis=0, tiled=True),
        lax.all_gather(conv_weight, "shard", axis=0, tiled=True),
        lax.all_gather(conv_bias, "shard", axis=0, tiled=True),
        lax.all_gather(gate_norm_weight, "shard", axis=0, tiled=True),
        lax.all_gather(out_weight, "shard", axis=0, tiled=True),
    )
    norm_full, in_full, conv_full, shift_full, gate_full, out_full = gathered
    valid = length_row[rank]
    keep = (jnp.arange(seq_len, dtype=jnp.int32) < valid).astype(jnp.float32)
    forward_out, saved = forward_seq(
        got_tokens[0, 0].astype(jnp.float32),
        keep,
        norm_full,
        in_full,
        conv_full,
        shift_full,
        gate_full,
        out_full,
        step_bias,
        decay_log,
        skip_gain,
    )
    result = forward_out[None]
    grad_seq, weight_grads, head_terms = backward_seq(
        saved, got_cot[0, 0].astype(jnp.float32), in_full, out_full
    )
    input_grad = grad_seq[None]
    back_out, back_grad = (
        lax.all_to_all(result, "shard", split_axis=1, concat_axis=0, tiled=True),
        lax.all_to_all(input_grad, "shard", split_axis=1, concat_axis=0, tiled=True),
    )
    output = jnp.take(back_out, order_row, axis=0)
    input_back = jnp.take(back_grad, order_row, axis=0)
    summed = lax.psum(
        (
            weight_grads[0],
            weight_grads[1],
            weight_grads[2],
            weight_grads[3],
            weight_grads[4],
            weight_grads[5],
        ),
        "rep",
    )
    pieces = (
        lax.psum_scatter(summed[0], "shard", scatter_dimension=0, tiled=True),
        lax.psum_scatter(summed[1], "shard", scatter_dimension=0, tiled=True),
        lax.psum_scatter(summed[2], "shard", scatter_dimension=0, tiled=True),
        lax.psum_scatter(summed[3], "shard", scatter_dimension=0, tiled=True),
        lax.psum_scatter(summed[4], "shard", scatter_dimension=0, tiled=True),
        lax.psum_scatter(summed[5], "shard", scatter_dimension=0, tiled=True),
    )
    head_sums = lax.psum((head_terms[0], head_terms[1], head_terms[2]), ("rep", "shard"))
    return (
        output,
        input_back,
        pieces[0],
        pieces[1],
        pieces[2],
        pieces[3],
        head_sums[0],
        head_sums[1],
        head_sums[2],
        pieces[4],
        pieces[5],
    )


def solution(mesh):
    placed = (
        P("rep", "shard", None),
        P("rep", "shard", None),
        P("rep", None),
        P("rep", None),
        P("shard"),
        P("shard", None),
        P("shard", None),
        P("shard"),
        P(),
        P(),
        P(),
        P("shard"),
        P("shard", None),
    )
    return jax.shard_map(
        on_device,
        mesh=mesh,
        in_specs=placed,
        out_specs=(
            P("rep", "shard", None),
            P("rep", "shard", None),
            P("shard"),
            P("shard", None),
            P("shard", None),
            P("shard"),
            P(),
            P(),
            P(),
            P("shard"),
            P("shard", None),
        ),
        check_vma=False,
    )
```

profile of v0, /device:TPU:0, one launch (start us, length us, event | category | flops | bytes accessed | tf_op | source)
XLA Modules:
  0.0 1286.4 jit_solution(3603219273039151114)
XLA Ops:
  15.6 65.5 %all_to_all.42 = bf16[16,1,64,768]{3,2,1,0:T(8,128)(2,1)S(1)} all-to-all(bf16[16,1,64,768]{3,2,1,0:T(8,128)(2,1)S(1)} %get-tuple-element.698), channel_id=1, replica_groups=mesh['rep'=2,'shard'=16] {'shard'}, dimensions={0} | all-to-all | bytes 3145728 | tf_op jit(solution)/shard_map/all_to_all | solution.py:243
  81.1 4.5 all-to-all-start.2
  89.8 115.9 %all-reduce.21 = (bf16[768]{0:T(1024)(128)(2,1)S(1)}, bf16[1792]{0:T(1024)(128)(2,1)S(1)}, bf16[1536]{0:T(1024)(128)(2,1)S(1)}) all-reduce(bf16[768]{0:T(1024)(128)(2,1)S(1)} %dynamic-update-slice, bf16[1792]{0:T(1024)(128)(2,1)S(1)} %dynamic-update-slice.1, ...), channel_id=1, replica_groups=mesh['rep'=2,'shard'=16] {'shard'}, use_global_device_ids=true, to_apply=%add.11 | all-reduce | flops 4096 | bytes 16384
  205.8 35.7 %all-gather = bf16[16,112,4]{1,2,0:T(4,128)(2,1)S(1)} all-gather(bf16[1,112,4]{1,2,0:T(4,128)(2,1)S(1)} %bitcast.455), channel_id=1, replica_groups=mesh['rep'=2,'shard'=16] {'shard'}, dimensions={0}, use_global_device_ids=true | all-gather | bytes 15232 | tf_op jit(solution)/shard_map/all_gather | solution.py:251
  248.1 11.4 fusion.140
  259.5 3.8 slice.133
  263.3 10.1 fusion.136
  278.4 6.2 reshape.413
  284.6 4.1 copy.211
  293.2 4.0 broadcast.186.clone2
  297.2 182.0 %while.40 = (s32[]{:T(128)}, f32[24,64,128]{2,1,0:T(8,128)S(1)}, f32[4,256,24,64]{1,0,3,2:T(4,128)}, f32[4,24,64,128]{3,2,1,0:T(8,128)}, f32[4,256,24]{1,2,0:T(8...) while((s32[]{:T(128)}, f32[24,64,128]{2,1,0:T(8,128)S(1)}, ...), condition=%wide.region_5.7_spmd.clone, body=%wide.region_2.0_spmd.clone.sunk | while | flops 432687168 | bytes 17880888 | solution.py:153
  300.7 3.4 fusion.191
  305.7 34.5 %dynamic_update_slice.73 = f32[4,256,24,64]{1,0,3,2:T(4,128)} dynamic-update-slice(f32[4,256,24,64]{1,0,3,2:T(4,128)} %get-tuple-element.896, f32[1,256,24,64]{1,0,3,2:T(1,128)S(1)} %copy.355, s32[]{:T(128)} %get-tuple-element.894, s32[]{:T(128)} %constant.126.clone.1..sunk, s32[]{:T(128)} %constant.126.clone.1..sunk, s32[]{:T(128)} %constant.126.clone.1..sunk) | dynamic-update-slice | bytes 3145732 | tf_op jit(solution)/shard_map/while/body/jit(dynamic_update_index_in_dim)/dynamic_update_slice | solution.py:153
  346.2 3.4 fusion.191
  351.2 34.5 %dynamic_update_slice.73 = f32[4,256,24,64]{1,0,3,2:T(4,128)} dynamic-update-slice(f32[4,256,24,64]{1,0,3,2:T(4,128)} %get-tuple-element.896, f32[1,256,24,64]{1,0,3,2:T(1,128)S(1)} %copy.355, s32[]{:T(128)} %get-tuple-element.894, s32[]{:T(128)} %constant.126.clone.1..sunk, s32[]{:T(128)} %constant.126.clone.1..sunk, s32[]{:T(128)} %constant.126.clone.1..sunk) | dynamic-update-slice | bytes 3145732 | tf_op jit(solution)/shard_map/while/body/jit(dynamic_update_index_in_dim)/dynamic_update_slice | solution.py:153
  391.6 3.4 fusion.191
  396.6 34.5 %dynamic_update_slice.73 = f32[4,256,24,64]{1,0,3,2:T(4,128)} dynamic-update-slice(f32[4,256,24,64]{1,0,3,2:T(4,128)} %get-tuple-element.896, f32[1,256,24,64]{1,0,3,2:T(1,128)S(1)} %copy.355, s32[]{:T(128)} %get-tuple-element.894, s32[]{:T(128)} %constant.126.clone.1..sunk, s32[]{:T(128)} %constant.126.clone.1..sunk, s32[]{:T(128)} %constant.126.clone.1..sunk) | dynamic-update-slice | bytes 3145732 | tf_op jit(solution)/shard_map/while/body/jit(dynamic_update_index_in_dim)/dynamic_update_slice | solution.py:153
  437.1 3.4 fusion.191
  442.1 34.5 %dynamic_update_slice.73 = f32[4,256,24,64]{1,0,3,2:T(4,128)} dynamic-update-slice(f32[4,256,24,64]{1,0,3,2:T(4,128)} %get-tuple-element.896, f32[1,256,24,64]{1,0,3,2:T(1,128)S(1)} %copy.355, s32[]{:T(128)} %get-tuple-element.894, s32[]{:T(128)} %constant.126.clone.1..sunk, s32[]{:T(128)} %constant.126.clone.1..sunk, s32[]{:T(128)} %constant.126.clone.1..sunk) | dynamic-update-slice | bytes 3145732 | tf_op jit(solution)/shard_map/while/body/jit(dynamic_update_index_in_dim)/dynamic_update_slice | solution.py:153
  479.2 4.3 copy.281
  483.6 8.3 multiply_reduce_fusion.9
  494.5 4.6 fusion.130
  499.0 7.8 multiply_reduce_fusion.6
  506.9 14.3 %multiply_reduce_fusion.7 = (f32[1536]{0:T(1024)}, f32[1024,1536]{0,1:T(8,128)}, bf16[1024,1536]{0,1:T(8,128)(2,1)}) fusion(f32[1024,1792]{0,1:T(8,128)} %copy-done.2, f32[1024,3352]{0,1:T(8,128)} %fusion.140, f32[1024,1536]{0,1:T(8,128)S(1)} %copy-done.8, f32[1024]{0:T(1024)S(1)} %multiply_multiply_fusion.1, f32[1024]{0:T(1024)S(1)} %fusion.127, ...), kind=kLoop, calls=%fused_computation.179 | loop fusion | flops 34601472 | bytes 40921088 | tf_op jit(solution)/shard_map/transpose(jvp())/reduce_sum | solution.py:52
  521.2 8.1 reshape.419
  529.3 4.1 broadcast.186.clone
  536.4 292.3 %while.41 = (s32[]{:T(128)}, f32[24,64,128]{2,1,0:T(8,128)S(1)}, f32[4,256,24,64]{1,0,3,2:T(4,128)}, f32[4,256,128]{2,1,0:T(8,128)}, f32[4,256,128]{2,1,0:T(8,12...) while((s32[]{:T(128)}, f32[24,64,128]{2,1,0:T(8,128)S(1)}, ...), condition=%wide.region_21.23_spmd.clone, body=%wide.region_8.22_spmd.clone.sunk | while | flops 998139968 | bytes 33770432 | solution.py:177
  539.0 4.5 constant_dynamic-slice_fusion.3
  543.6 6.0 fusion.207
  555.9 3.8 fusion.212
  562.6 34.8 %dynamic_update_slice.76 = f32[4,256,24,64]{1,0,3,2:T(4,128)} dynamic-update-slice(f32[4,256,24,64]{1,0,3,2:T(4,128)} %get-tuple-element.938, f32[1,256,24,64]{1,0,3,2:T(1,128)} %copy.368, s32[]{:T(128)S(6)} %sub.232, s32[]{:T(128)} %constant.126.clone.1..sunk.1, s32[]{:T(128)} %constant.126.clone.1..sunk.1, s32[]{:T(128)} %constant.126.clone.1..sunk.1) | dynamic-update-slice | bytes 3145732 | tf_op jit(solution)/shard_map/while/body/jit(dynamic_update_index_in_dim)/dynamic_update_slice | solution.py:153
  612.2 4.5 constant_dynamic-slice_fusion.3
  616.7 6.0 fusion.207
  629.1 3.7 fusion.212
  635.7 34.7 %dynamic_update_slice.76 = f32[4,256,24,64]{1,0,3,2:T(4,128)} dynamic-update-slice(f32[4,256,24,64]{1,0,3,2:T(4,128)} %get-tuple-element.938, f32[1,256,24,64]{1,0,3,2:T(1,128)} %copy.368, s32[]{:T(128)S(6)} %sub.232, s32[]{:T(128)} %constant.126.clone.1..sunk.1, s32[]{:T(128)} %constant.126.clone.1..sunk.1, s32[]{:T(128)} %constant.126.clone.1..sunk.1) | dynamic-update-slice | bytes 3145732 | tf_op jit(solution)/shard_map/while/body/jit(dynamic_update_index_in_dim)/dynamic_update_slice | solution.py:153
  685.3 4.5 constant_dynamic-slice_fusion.3
  689.8 6.0 fusion.207
  702.1 3.7 fusion.212
  708.7 34.7 %dynamic_update_slice.76 = f32[4,256,24,64]{1,0,3,2:T(4,128)} dynamic-update-slice(f32[4,256,24,64]{1,0,3,2:T(4,128)} %get-tuple-element.938, f32[1,256,24,64]{1,0,3,2:T(1,128)} %copy.368, s32[]{:T(128)S(6)} %sub.232, s32[]{:T(128)} %constant.126.clone.1..sunk.1, s32[]{:T(128)} %constant.126.clone.1..sunk.1, s32[]{:T(128)} %constant.126.clone.1..sunk.1) | dynamic-update-slice | bytes 3145732 | tf_op jit(solution)/shard_map/while/body/jit(dynamic_update_index_in_dim)/dynamic_update_slice | solution.py:153
  758.3 4.5 constant_dynamic-slice_fusion.3
  762.8 6.0 fusion.207
  775.1 3.7 fusion.212
  781.7 34.7 %dynamic_update_slice.76 = f32[4,256,24,64]{1,0,3,2:T(4,128)} dynamic-update-slice(f32[4,256,24,64]{1,0,3,2:T(4,128)} %get-tuple-element.938, f32[1,256,24,64]{1,0,3,2:T(1,128)} %copy.368, s32[]{:T(128)S(6)} %sub.232, s32[]{:T(128)} %constant.126.clone.1..sunk.1, s32[]{:T(128)} %constant.126.clone.1..sunk.1, s32[]{:T(128)} %constant.126.clone.1..sunk.1) | dynamic-update-slice | bytes 3145732 | tf_op jit(solution)/shard_map/while/body/jit(dynamic_update_index_in_dim)/dynamic_update_slice | solution.py:153
  830.6 7.0 copy.282
  839.2 5.3 multiply_add_fusion.1
  844.6 19.0 %multiply_reduce_fusion.4 = (f32[1792]{0:T(1024)S(1)}, f32[1792]{0:T(1024)S(1)}, f32[1792]{0:T(1024)S(1)}, f32[1792]{0:T(1024)S(1)}, f32[1792]{0:T(1024)S(1)}, /*index=5*/f32[1024,1792]{0,1:T(8,128)S(1)}) fusion(f32[1024,1792]{0,1:T(8,128)} %copy-done.3, f32[1024,3352]{0,1:T(8,128)} %fusion.140, f32[1024,1792]{0,1:T(8,128)} %get-tuple-element.668, ...), kind=kLoop, calls=%fused_computation.169 | loop fusion | flops 36691200 | bytes 36736000 | tf_op jit(solution)/shard_map/transpose(jvp())/reduce_sum | solution.py:42
  863.6 8.5 broadcast_multiply_fusion
  872.1 12.1 fusion.103
  884.3 12.9 %fusion.119 = f32[768,3352]{1,0:T(8,128)} fusion(bf16[1024,768]{1,0:T(8,128)(2,1)S(1)} %copy-done.11, bf16[1024,24]{0,1:T(8,128)(2,1)S(1)} %get-tuple-element.662, bf16[1024,1792]{0,1:T(8,128)(2,1)} %fusion.103, bf16[1024,1536]{0,1:T(8,128)(2,1)} %get-tuple-element.685), kind=kOutput, calls=%fused_computation.210 | convolution fusion | flops 5292834816 | bytes 18735104 | tf_op jit(solution)/shard_map/ti,tj->ij/dot_general | solution.py:199
  898.6 6.4 fusion.121
  905.0 4.1 copy.331
  909.6 11.7 reduce.22
  922.6 3.7 all-to-all-start.1
  926.4 10.7 fusion.114
  939.4 4.2 copy.330
  943.6 11.5 reduce.21
  956.5 20.8 %all-to-all-done.1 = bf16[16,2,24576]{2,1,0:T(2,128)(2,1)S(1)} async-done(((bf16[16,2,24576]{2,1,0:T(2,128)(2,1)}), bf16[16,2,24576]{2,1,0:T(2,128)(2,1)S(1)}, u32[]{:S(2)}, u32[]{:S(2)}) %all-to-all-start.1) | async-done | bytes 1572896 | tf_op jit(solution)/shard_map/all_to_all | solution.py:278
  977.2 27.4 %all-to-all-start.3 = ((bf16[16,2,24576]{2,1,0:T(2,128)(2,1)}), bf16[16,2,24576]{2,1,0:T(2,128)(2,1)S(1)}, u32[]{:S(2)}, u32[]{:S(2)}) async-start(bf16[16,2,24576]{2,1,0:T(2,128)(2,1)} %reshape.519), calls=%async_computation.3 | async-start | bytes 3145728 | tf_op jit(solution)/shard_map/all_to_all | solution.py:279
  1008.1 122.2 %reduce-scatter.6.cloned.1.call-done = f32[48,3352]{1,0:T(8,128)} async-done(((f32[768,3352]{1,0:T(8,128)}), f32[48,3352]{1,0:T(8,128)}) %reduce-scatter.6.cloned.1.call-update) | async-done | bytes 643600 | tf_op jit(solution)/shard_map/reduce_scatter | solution.py:296
  1130.6 40.0 %all-reduce.17 = (f32[24]{0:T(128)}, f32[24]{0:T(128)}, f32[24]{0:T(128)}) all-reduce(f32[24]{0:T(128)S(1)} %get-tuple-element.661, f32[24]{0:T(128)S(1)} %negate_multiply_fusion, f32[24]{0:T(128)S(1)} %reduce_sum.344), channel_id=1, replica_groups=mesh['rep'=2,'shard'=16] {'rep','shard'}, use_global_device_ids=true, to_apply=%region_38.40 | all-reduce | flops 72 | bytes 576 | tf_op jit(solution)/shard_map/psum | solution.py:302
  1170.6 75.7 %all-reduce.18 = (f32[768]{0:T(1024)S(1)}, f32[1792]{0:T(1024)S(1)}, f32[1536]{0:T(1024)S(1)}) all-reduce(f32[768]{0:T(1024)S(1)} %get-tuple-element.592, f32[1792]{0:T(1024)S(1)} %get-tuple-element.590, f32[1536]{0:T(1024)S(1)} %copy-done.36), channel_id=2, replica_groups=mesh['rep'=2,'shard'=16] {'shard'}, use_global_device_ids=true, to_apply=%region_25.27.clone | all-reduce | flops 4096 | bytes 32768
  1250.4 6.3 reshape.518
  1258.8 6.3 reshape.520
  1272.2 3.4 broadcast_select_fusion
  (400 shorter events, 186.9 us)
Async XLA Ops:
  7.2 1.5 copy-start
  7.2 240.9 %all-gather.4.cloned.1.call-start = ((), (), s32[]{:S(2)}) async-start(), calls=%async_computation.7 | async-start | bytes 5640192 | tf_op jit(solution)/shard_map/all_gather | solution.py:250
  12.6 73.9 %copy-start.41 = (u32[32]{0:T(128)S(1)}, u32[32]{0:T(128)}, u32[]{:S(2)}) copy-start(u32[32]{0:T(128)} %constant.162) | copy-start | bytes 388
  12.6 76.5 %copy-start.44 = (bf16[112]{0:T(256)(128)(2,1)S(1)}, bf16[112]{0:T(256)(128)(2,1)}, u32[]{:S(2)}) copy-start(bf16[112]{0:T(256)(128)(2,1)} %param.26) | copy-start | bytes 676
  12.6 76.7 %copy-start.45 = (bf16[96]{0:T(256)(128)(2,1)S(1)}, bf16[96]{0:T(256)(128)(2,1)}, u32[]{:S(2)}) copy-start(bf16[96]{0:T(256)(128)(2,1)} %param.30) | copy-start | bytes 580
  12.6 77.0 %copy-start.46 = (bf16[48]{0:T(256)(128)(2,1)S(1)}, bf16[48]{0:T(256)(128)(2,1)}, u32[]{:S(2)}) copy-start(bf16[48]{0:T(256)(128)(2,1)} %param.23) | copy-start | bytes 292
  12.6 193.1 %copy-start.42 = (bf16[112,4]{0,1:T(4,128)(2,1)S(1)}, bf16[112,4]{0,1:T(4,128)(2,1)}, u32[]{:S(2)}) copy-start(bf16[112,4]{0,1:T(4,128)(2,1)} %param.25) | copy-start | bytes 2692
  12.6 228.9 %copy-start.43 = (f32[24]{0:T(128)S(1)}, f32[24]{0:T(128)}, u32[]{:S(2)}) copy-start(f32[24]{0:T(128)} %param.29) | copy-start | bytes 292
  12.7 229.0 %copy-start.47 = (s32[1,16]{1,0:T(1,128)S(1)}, s32[1,16]{1,0:T(1,128)}, u32[]{:S(2)}) copy-start(s32[1,16]{1,0:T(1,128)} %param.21) | copy-start | bytes 196
  12.7 230.4 %copy-start.49 = (f32[24]{0:T(128)S(1)}, f32[24]{0:T(128)}, u32[]{:S(2)}) copy-start(f32[24]{0:T(128)} %param.28) | copy-start | bytes 292
  81.1 178.3 %copy-start.5 = (bf16[16,1,64,768]{3,2,1,0:T(8,128)(2,1)}, bf16[16,1,64,768]{3,2,1,0:T(8,128)(2,1)S(1)}, u32[]{:S(2)}) copy-start(bf16[16,1,64,768]{3,2,1,0:T(8,128)(2,1)S(1)} %all_to_all.42) | copy-start | bytes 4718596
  81.1 164.1 %all-to-all-start.2 = ((bf16[16,1,64,768]{3,2,1,0:T(8,128)(2,1)}), bf16[16,1,64,768]{3,2,1,0:T(8,128)(2,1)}, u32[]{:S(2)}, u32[]{:S(2)}) async-start(bf16[16,1,64,768]{3,2,1,0:T(8,128)(2,1)} %get-tuple-element.697), calls=%async_computation.2 | async-start | bytes 3145728 | tf_op jit(solution)/shard_map/all_to_all | solution.py:244
  85.6 413.4 %all-gather.6.cloned.1.call-start = ((), (), s32[]{:S(2)}) async-start(), calls=%async_computation.8 | async-start | bytes 2506752 | tf_op jit(solution)/shard_map/all_gather | solution.py:254
  86.4 921.7 %reduce-scatter.8.cloned.1.call-start = ((), (), s32[]{:S(2)}) async-start(), calls=%async_computation.10 | async-start | bytes 5013504 | tf_op jit(solution)/shard_map/reduce_scatter | solution.py:300
  205.8 53.7 %copy-start.23 = (f32[768]{0:T(1024)}, f32[768]{0:T(1024)S(1)}, u32[]{:S(2)}) copy-start(f32[768]{0:T(1024)S(1)} %convert_element_type.160) | copy-start | bytes 9220
  241.7 265.1 %copy-start.29 = (f32[1536]{0:T(1024)}, f32[1536]{0:T(1024)S(1)}, u32[]{:S(2)}) copy-start(f32[1536]{0:T(1024)S(1)} %convert_element_type.165) | copy-start | bytes 18436
  242.9 16.5 %copy-start.32 = (f32[1024]{0:T(1024)}, f32[1024]{0:T(1024)S(1)}, u32[]{:S(2)}) copy-start(f32[1024]{0:T(1024)S(1)} %fusion.126) | copy-start | bytes 12292
  243.0 20.2 %copy-start.15 = (f32[1792]{0:T(1024)}, f32[1792]{0:T(1024)S(1)}, u32[]{:S(2)}) copy-start(f32[1792]{0:T(1024)S(1)} %get-tuple-element.594) | copy-start | bytes 21508
  243.1 20.2 %copy-start.17 = (f32[1792]{0:T(1024)}, f32[1792]{0:T(1024)S(1)}, u32[]{:S(2)}) copy-start(f32[1792]{0:T(1024)S(1)} %get-tuple-element.595) | copy-start | bytes 21508
  243.1 20.2 %copy-start.19 = (f32[1792]{0:T(1024)}, f32[1792]{0:T(1024)S(1)}, u32[]{:S(2)}) copy-start(f32[1792]{0:T(1024)S(1)} %get-tuple-element.596) | copy-start | bytes 21508
  243.1 20.2 %copy-start.21 = (f32[1792]{0:T(1024)}, f32[1792]{0:T(1024)S(1)}, u32[]{:S(2)}) copy-start(f32[1792]{0:T(1024)S(1)} %get-tuple-element.597) | copy-start | bytes 21508
  243.1 47.7 %copy-start.39 = (f32[24]{0:T(128)}, f32[24]{0:T(128)S(1)}, u32[]{:S(2)}) copy-start(f32[24]{0:T(128)S(1)} %exponential_negate_fusion) | copy-start | bytes 292
  243.6 15.9 %copy-start.27 = (f32[1024]{0:T(1024)}, f32[1024]{0:T(1024)S(1)}, u32[]{:S(2)}) copy-start(f32[1024]{0:T(1024)S(1)} %add.193) | copy-start | bytes 12292
  243.6 15.9 %copy-start.25 = (f32[1024]{0:T(1024)}, f32[1024]{0:T(1024)S(1)}, u32[]{:S(2)}) copy-start(f32[1024]{0:T(1024)S(1)} %rsqrt.20) | copy-start | bytes 12292
  263.3 10.1 copy-start.3
  273.4 2.9 copy-start.2
  278.4 12.4 copy-start.37
  291.9 0.6 copy-start.13
  483.5 8.3 copy-start.4
  483.6 10.9 copy-start.12
  491.9 2.6 copy-start.7
  491.9 14.9 %copy-start.34 = (f32[1024]{0:T(1024)}, f32[1024]{0:T(1024)S(1)}, u32[]{:S(2)}) copy-start(f32[1024]{0:T(1024)S(1)} %fusion.127) | copy-start | bytes 12292
  499.0 7.8 copy-start.8
  529.3 601.0 %reduce-scatter.6.cloned.1.call-start = ((), (), s32[]{:S(2)}) async-start(), calls=%async_computation.9 | async-start | bytes 11280384 | tf_op jit(solution)/shard_map/reduce_scatter | solution.py:296
  830.6 7.1 copy-start.9
  830.6 7.3 copy-start.10
  830.6 7.5 copy-start.14
  830.6 7.5 copy-start.38
  830.6 7.5 copy-start.40
  844.5 19.0 %copy-start.16 = (f32[1792]{0:T(1024)S(1)}, f32[1792]{0:T(1024)}, u32[]{:S(2)}) copy-start(f32[1792]{0:T(1024)} %copy-done.15) | copy-start | bytes 21508
  844.5 19.0 %copy-start.18 = (f32[1792]{0:T(1024)S(1)}, f32[1792]{0:T(1024)}, u32[]{:S(2)}) copy-start(f32[1792]{0:T(1024)} %copy-done.17) | copy-start | bytes 21508
  844.6 19.0 %copy-start.20 = (f32[1792]{0:T(1024)S(1)}, f32[1792]{0:T(1024)}, u32[]{:S(2)}) copy-start(f32[1792]{0:T(1024)} %copy-done.19) | copy-start | bytes 21508
  844.6 19.0 %copy-start.22 = (f32[1792]{0:T(1024)S(1)}, f32[1792]{0:T(1024)}, u32[]{:S(2)}) copy-start(f32[1792]{0:T(1024)} %copy-done.21) | copy-start | bytes 21508
  872.1 12.1 copy-start.11
  897.2 1.4 copy-start.6
  897.2 1.4 copy-start.30
  897.2 1.4 copy-start.33
  897.2 1.4 copy-start.35
  909.1 17.2 %copy-start.24 = (f32[768]{0:T(1024)S(1)}, f32[768]{0:T(1024)}, u32[]{:S(2)}) copy-start(f32[768]{0:T(1024)} %copy-done.23) | copy-start | bytes 9220
  909.1 17.2 %copy-start.26 = (f32[1024]{0:T(1024)S(1)}, f32[1024]{0:T(1024)}, u32[]{:S(2)}) copy-start(f32[1024]{0:T(1024)} %copy-done.25) | copy-start | bytes 12292
  922.6 54.6 %all-to-all-start.1 = ((bf16[16,2,24576]{2,1,0:T(2,128)(2,1)}), bf16[16,2,24576]{2,1,0:T(2,128)(2,1)S(1)}, u32[]{:S(2)}, u32[]{:S(2)}) async-start(bf16[16,2,24576]{2,1,0:T(2,128)(2,1)} %reshape.517), calls=%async_computation.1 | async-start | bytes 3145728 | tf_op jit(solution)/shard_map/all_to_all | solution.py:278
  926.3 10.7 copy-start.28
  943.6 62.5 %copy-start.48 = (s32[1,16]{1,0:T(1,128)S(1)}, s32[1,16]{1,0:T(1,128)}, u32[]{:S(2)}) copy-start(s32[1,16]{1,0:T(1,128)} %param.22) | copy-start | bytes 196
  943.6 186.8 %copy-start.31 = (f32[1536]{0:T(1024)S(1)}, f32[1536]{0:T(1024)}, u32[]{:S(2)}) copy-start(f32[1536]{0:T(1024)} %get-tuple-element.659) | copy-start | bytes 18436
  943.6 187.0 %copy-start.50 = (f32[24]{0:T(128)S(1)}, f32[24]{0:T(128)}, u32[]{:S(2)}) copy-start(f32[24]{0:T(128)} %param.28) | copy-start | bytes 292
  943.6 227.0 %copy-start.36 = (f32[1536]{0:T(1024)S(1)}, f32[1536]{0:T(1024)}, u32[]{:S(2)}) copy-start(f32[1536]{0:T(1024)} %get-tuple-element.588) | copy-start | bytes 18436
  977.2 281.6 %all-to-all-start.3 = ((bf16[16,2,24576]{2,1,0:T(2,128)(2,1)}), bf16[16,2,24576]{2,1,0:T(2,128)(2,1)S(1)}, u32[]{:S(2)}, u32[]{:S(2)}) async-start(bf16[16,2,24576]{2,1,0:T(2,128)(2,1)} %reshape.519), calls=%async_computation.3 | async-start | bytes 3145728 | tf_op jit(solution)/shard_map/all_to_all | solution.py:279
  1004.6 241.9 %reduce-scatter.10.cloned.1.call-start = ((), (), s32[]{:S(2)}) async-start(), calls=%async_computation.11 | async-start | bytes 974848
  1006.1 269.6 %all-reduce.24.cloned.1.call-start = ((), (), s32[]{:S(2)}) async-start(), calls=%async_computation.12 | async-start | bytes 1916928 | tf_op jit(solution)/shard_map/psum | solution.py:283
  1268.4 10.9 copy-start.1
Sparse Core Ops, SparseCore 0:
  10.8 132.4 all-gather.3
  146.1 62.0 all-gather.5
  529.4 135.1 reduce-scatter.7
  897.3 232.9 reduce-scatter.5
  1133.0 76.8 reduce-scatter.9
  1212.3 15.8 all-reduce.23
where the time goes:
time: 1300 us; the launch traced here: 1290 us
  local copies, waits for them, and re-layouts  440 us (34%)
  blocking collectives  336 us (26%)
  matrix products  164 us (13%)
  other arithmetic  146 us (11%)
  waiting for transfers between devices  144 us (11%)
  starting transfers between devices  35.8 us (3%)
  between operations  19.1 us (1%)
    dynamic_update_slice x16, local copies, waits for them, and re-layouts, forward_seq(): final_state, kept = lax.scan(block_forward, start, blocks)  295 us
    unnamed x2, blocking collectives  192 us
    reduce_scatter x1, waiting for transfers between devices, on_device(): lax.psum_scatter(summed[1], 'shard', scatter_dimension=0, tiled=True)  122 us
    all_to_all x1, blocking collectives, on_device(): lax.all_to_all(sent_tokens, 'shard', split_axis=0, concat_axis=2, tiled=T...  65.5 us
    unnamed x131, local copies, waits for them, and re-layouts  55.2 us
    psum x1, blocking collectives, on_device(): lax.psum((head_terms[0], head_terms[1], head_terms[2]), ('rep', 'shard'))  40 us
    another operation x34, other arithmetic  37.8 us
    all_gather x1, blocking collectives, on_device(): lax.all_gather(conv_weight, 'shard', axis=0, tiled=True)  35.7 us
  transfers between devices with their start and end apart: 9, of which 2 were waited for; matrix products, arithmetic and copies ran while one was open for 55% of the time, Pallas kernels for 0%

commit v1 on v0

--- a/solution.py
+++ b/solution.py
@@ -299,7 +299,7 @@
         lax.psum_scatter(summed[4], "shard", scatter_dimension=0, tiled=True),
         lax.psum_scatter(summed[5], "shard", scatter_dimension=0, tiled=True),
     )
-    head_sums = lax.psum((head_terms[0], head_terms[1], head_terms[2]), ("rep", "shard"))
+    head_sums = lax.psum(lax.psum((head_terms[0], head_terms[1], head_terms[2]), "shard"), "rep")
     return (
         output,
         input_back,

time: 1300 us -> 1260 us (0.969)
  blocking collectives: 336 us -> 295 us
    psum x1 -> x0, blocking collectives: 40 us -> none  [on_device(): lax.psum((head_terms[0], head_terms[1], head_terms[2]), ('rep', 'shard'))]
    unnamed x131 -> x135, local copies, waits for them, and re-layouts: 55.2 us -> 53.4 us
  transfers between devices with their start and end apart: 9 -> 9, of which waited for: 2 -> 3; matrix products, arithmetic and copies ran while one was open for 55% -> 57% of each run, Pallas kernels for 0% -> 0%
where the time goes in v1:
time: 1260 us; the launch traced here: 1250 us
  local copies, waits for them, and re-layouts  439 us (35%)
  blocking collectives  295 us (23%)
  matrix products  164 us (13%)
  waiting for transfers between devices  148 us (12%)
  other arithmetic  146 us (12%)
  starting transfers between devices  35.8 us (3%)
  between operations  19.2 us (2%)
    dynamic_update_slice x16, local copies, waits for them, and re-layouts, forward_seq(): final_state, kept = lax.scan(block_forward, start, blocks)  295 us
    unnamed x2, blocking collectives  191 us
    reduce_scatter x1, waiting for transfers between devices, on_device(): lax.psum_scatter(summed[1], 'shard', scatter_dimension=0, tiled=True)  122 us
    all_to_all x1, blocking collectives, on_device(): lax.all_to_all(sent_tokens, 'shard', split_axis=0, concat_axis=2, tiled=T...  65.5 us
    unnamed x135, local copies, waits for them, and re-layouts  53.4 us
    another operation x34, other arithmetic  37.8 us
    all_gather x1, blocking collectives, on_device(): lax.all_gather(conv_weight, 'shard', axis=0, tiled=True)  35.7 us
    all_to_all x1, starting transfers between devices, on_device(): lax.all_to_all(input_grad, 'shard', split_axis=1, concat_axis=0, tiled=True)  27.4 us
  transfers between devices with their start and end apart: 9, of which 3 were waited for; matrix products, arithmetic and copies ran while one was open for 57% of the time, Pallas kernels for 0%

profile of v1, /device:TPU:0, one launch (start us, length us, event | category | flops | bytes accessed | tf_op | source)
XLA Modules:
  0.0 1248.1 jit_solution(8299810193421568275)
XLA Ops:
  15.6 65.5 %all_to_all.42 = bf16[16,1,64,768]{3,2,1,0:T(8,128)(2,1)S(1)} all-to-all(bf16[16,1,64,768]{3,2,1,0:T(8,128)(2,1)S(1)} %get-tuple-element.701), channel_id=1, replica_groups=mesh['rep'=2,'shard'=16] {'shard'}, dimensions={0} | all-to-all | bytes 3145728 | tf_op jit(solution)/shard_map/all_to_all | solution.py:243
  81.1 4.5 all-to-all-start.2
  89.8 115.9 %all-reduce.20 = (bf16[768]{0:T(1024)(128)(2,1)S(1)}, bf16[1792]{0:T(1024)(128)(2,1)S(1)}, bf16[1536]{0:T(1024)(128)(2,1)S(1)}) all-reduce(bf16[768]{0:T(1024)(128)(2,1)S(1)} %dynamic-update-slice, bf16[1792]{0:T(1024)(128)(2,1)S(1)} %dynamic-update-slice.1, ...), channel_id=1, replica_groups=mesh['rep'=2,'shard'=16] {'shard'}, use_global_device_ids=true, to_apply=%add.11 | all-reduce | flops 4096 | bytes 16384
  205.8 35.7 %all-gather = bf16[16,112,4]{1,2,0:T(4,128)(2,1)S(1)} all-gather(bf16[1,112,4]{1,2,0:T(4,128)(2,1)S(1)} %bitcast.455), channel_id=1, replica_groups=mesh['rep'=2,'shard'=16] {'shard'}, dimensions={0}, use_global_device_ids=true | all-gather | bytes 15232 | tf_op jit(solution)/shard_map/all_gather | solution.py:251
  248.1 11.4 fusion.140
  259.5 3.8 slice.133
  263.3 10.1 fusion.136
  278.4 6.2 reshape.413
  284.6 4.1 copy.211
  293.2 4.0 broadcast.186.clone2
  297.2 182.0 %while.40 = (s32[]{:T(128)}, f32[24,64,128]{2,1,0:T(8,128)S(1)}, f32[4,256,24,64]{1,0,3,2:T(4,128)}, f32[4,24,64,128]{3,2,1,0:T(8,128)}, f32[4,256,24]{1,2,0:T(8...) while((s32[]{:T(128)}, f32[24,64,128]{2,1,0:T(8,128)S(1)}, ...), condition=%wide.region_5.7_spmd.clone, body=%wide.region_2.0_spmd.clone.sunk | while | flops 432687168 | bytes 17880888 | solution.py:153
  300.7 3.4 fusion.191
  305.7 34.5 %dynamic_update_slice.73 = f32[4,256,24,64]{1,0,3,2:T(4,128)} dynamic-update-slice(f32[4,256,24,64]{1,0,3,2:T(4,128)} %get-tuple-element.899, f32[1,256,24,64]{1,0,3,2:T(1,128)S(1)} %copy.355, s32[]{:T(128)} %get-tuple-element.897, s32[]{:T(128)} %constant.126.clone.1..sunk, s32[]{:T(128)} %constant.126.clone.1..sunk, s32[]{:T(128)} %constant.126.clone.1..sunk) | dynamic-update-slice | bytes 3145732 | tf_op jit(solution)/shard_map/while/body/jit(dynamic_update_index_in_dim)/dynamic_update_slice | solution.py:153
  346.2 3.4 fusion.191
  351.2 34.5 %dynamic_update_slice.73 = f32[4,256,24,64]{1,0,3,2:T(4,128)} dynamic-update-slice(f32[4,256,24,64]{1,0,3,2:T(4,128)} %get-tuple-element.899, f32[1,256,24,64]{1,0,3,2:T(1,128)S(1)} %copy.355, s32[]{:T(128)} %get-tuple-element.897, s32[]{:T(128)} %constant.126.clone.1..sunk, s32[]{:T(128)} %constant.126.clone.1..sunk, s32[]{:T(128)} %constant.126.clone.1..sunk) | dynamic-update-slice | bytes 3145732 | tf_op jit(solution)/shard_map/while/body/jit(dynamic_update_index_in_dim)/dynamic_update_slice | solution.py:153
  391.6 3.4 fusion.191
  396.6 34.5 %dynamic_update_slice.73 = f32[4,256,24,64]{1,0,3,2:T(4,128)} dynamic-update-slice(f32[4,256,24,64]{1,0,3,2:T(4,128)} %get-tuple-element.899, f32[1,256,24,64]{1,0,3,2:T(1,128)S(1)} %copy.355, s32[]{:T(128)} %get-tuple-element.897, s32[]{:T(128)} %constant.126.clone.1..sunk, s32[]{:T(128)} %constant.126.clone.1..sunk, s32[]{:T(128)} %constant.126.clone.1..sunk) | dynamic-update-slice | bytes 3145732 | tf_op jit(solution)/shard_map/while/body/jit(dynamic_update_index_in_dim)/dynamic_update_slice | solution.py:153
  437.1 3.4 fusion.191
  442.1 34.5 %dynamic_update_slice.73 = f32[4,256,24,64]{1,0,3,2:T(4,128)} dynamic-update-slice(f32[4,256,24,64]{1,0,3,2:T(4,128)} %get-tuple-element.899, f32[1,256,24,64]{1,0,3,2:T(1,128)S(1)} %copy.355, s32[]{:T(128)} %get-tuple-element.897, s32[]{:T(128)} %constant.126.clone.1..sunk, s32[]{:T(128)} %constant.126.clone.1..sunk, s32[]{:T(128)} %constant.126.clone.1..sunk) | dynamic-update-slice | bytes 3145732 | tf_op jit(solution)/shard_map/while/body/jit(dynamic_update_index_in_dim)/dynamic_update_slice | solution.py:153
  479.2 4.3 copy.281
  483.6 8.3 multiply_reduce_fusion.9
  494.5 4.6 fusion.130
  499.0 7.8 multiply_reduce_fusion.6
  506.9 14.3 %multiply_reduce_fusion.7 = (f32[1536]{0:T(1024)}, f32[1024,1536]{0,1:T(8,128)}, bf16[1024,1536]{0,1:T(8,128)(2,1)}) fusion(f32[1024,1792]{0,1:T(8,128)} %copy-done.2, f32[1024,3352]{0,1:T(8,128)} %fusion.140, f32[1024,1536]{0,1:T(8,128)S(1)} %copy-done.8, f32[1024]{0:T(1024)S(1)} %multiply_multiply_fusion.1, f32[1024]{0:T(1024)S(1)} %fusion.127, ...), kind=kLoop, calls=%fused_computation.179 | loop fusion | flops 34601472 | bytes 40921088 | tf_op jit(solution)/shard_map/transpose(jvp())/reduce_sum | solution.py:52
  521.2 8.1 reshape.419
  529.3 4.1 broadcast.186.clone
  536.4 292.3 %while.41 = (s32[]{:T(128)}, f32[24,64,128]{2,1,0:T(8,128)S(1)}, f32[4,256,24,64]{1,0,3,2:T(4,128)}, f32[4,256,128]{2,1,0:T(8,128)}, f32[4,256,128]{2,1,0:T(8,12...) while((s32[]{:T(128)}, f32[24,64,128]{2,1,0:T(8,128)S(1)}, ...), condition=%wide.region_21.23_spmd.clone, body=%wide.region_8.22_spmd.clone.sunk | while | flops 998139968 | bytes 33770432 | solution.py:177
  539.0 4.5 constant_dynamic-slice_fusion.3
  543.6 6.0 fusion.207
  555.9 3.8 fusion.212
  562.6 34.8 %dynamic_update_slice.76 = f32[4,256,24,64]{1,0,3,2:T(4,128)} dynamic-update-slice(f32[4,256,24,64]{1,0,3,2:T(4,128)} %get-tuple-element.941, f32[1,256,24,64]{1,0,3,2:T(1,128)} %copy.368, s32[]{:T(128)S(6)} %sub.232, s32[]{:T(128)} %constant.126.clone.1..sunk.1, s32[]{:T(128)} %constant.126.clone.1..sunk.1, s32[]{:T(128)} %constant.126.clone.1..sunk.1) | dynamic-update-slice | bytes 3145732 | tf_op jit(solution)/shard_map/while/body/jit(dynamic_update_index_in_dim)/dynamic_update_slice | solution.py:153
  612.2 4.5 constant_dynamic-slice_fusion.3
  616.7 6.0 fusion.207
  629.1 3.7 fusion.212
  635.7 34.7 %dynamic_update_slice.76 = f32[4,256,24,64]{1,0,3,2:T(4,128)} dynamic-update-slice(f32[4,256,24,64]{1,0,3,2:T(4,128)} %get-tuple-element.941, f32[1,256,24,64]{1,0,3,2:T(1,128)} %copy.368, s32[]{:T(128)S(6)} %sub.232, s32[]{:T(128)} %constant.126.clone.1..sunk.1, s32[]{:T(128)} %constant.126.clone.1..sunk.1, s32[]{:T(128)} %constant.126.clone.1..sunk.1) | dynamic-update-slice | bytes 3145732 | tf_op jit(solution)/shard_map/while/body/jit(dynamic_update_index_in_dim)/dynamic_update_slice | solution.py:153
  685.3 4.5 constant_dynamic-slice_fusion.3
  689.8 6.0 fusion.207
  702.1 3.7 fusion.212
  708.7 34.7 %dynamic_update_slice.76 = f32[4,256,24,64]{1,0,3,2:T(4,128)} dynamic-update-slice(f32[4,256,24,64]{1,0,3,2:T(4,128)} %get-tuple-element.941, f32[1,256,24,64]{1,0,3,2:T(1,128)} %copy.368, s32[]{:T(128)S(6)} %sub.232, s32[]{:T(128)} %constant.126.clone.1..sunk.1, s32[]{:T(128)} %constant.126.clone.1..sunk.1, s32[]{:T(128)} %constant.126.clone.1..sunk.1) | dynamic-update-slice | bytes 3145732 | tf_op jit(solution)/shard_map/while/body/jit(dynamic_update_index_in_dim)/dynamic_update_slice | solution.py:153
  758.3 4.5 constant_dynamic-slice_fusion.3
  762.8 6.0 fusion.207
  775.1 3.7 fusion.212
  781.7 34.7 %dynamic_update_slice.76 = f32[4,256,24,64]{1,0,3,2:T(4,128)} dynamic-update-slice(f32[4,256,24,64]{1,0,3,2:T(4,128)} %get-tuple-element.941, f32[1,256,24,64]{1,0,3,2:T(1,128)} %copy.368, s32[]{:T(128)S(6)} %sub.232, s32[]{:T(128)} %constant.126.clone.1..sunk.1, s32[]{:T(128)} %constant.126.clone.1..sunk.1, s32[]{:T(128)} %constant.126.clone.1..sunk.1) | dynamic-update-slice | bytes 3145732 | tf_op jit(solution)/shard_map/while/body/jit(dynamic_update_index_in_dim)/dynamic_update_slice | solution.py:153
  828.8 7.0 copy.282
  837.5 5.3 multiply_add_fusion.1
  842.8 19.0 %multiply_reduce_fusion.4 = (f32[1792]{0:T(1024)S(1)}, f32[1792]{0:T(1024)S(1)}, f32[1792]{0:T(1024)S(1)}, f32[1792]{0:T(1024)S(1)}, f32[1792]{0:T(1024)S(1)}, /*index=5*/f32[1024,1792]{0,1:T(8,128)S(1)}) fusion(f32[1024,1792]{0,1:T(8,128)} %copy-done.3, f32[1024,3352]{0,1:T(8,128)} %fusion.140, f32[1024,1792]{0,1:T(8,128)} %get-tuple-element.671, ...), kind=kLoop, calls=%fused_computation.169 | loop fusion | flops 36691200 | bytes 36736000 | tf_op jit(solution)/shard_map/transpose(jvp())/reduce_sum | solution.py:42
  861.9 8.5 broadcast_multiply_fusion
  870.4 12.1 fusion.103
  882.5 12.9 %fusion.119 = f32[768,3352]{1,0:T(8,128)} fusion(bf16[1024,768]{1,0:T(8,128)(2,1)S(1)} %copy-done.11, bf16[1024,24]{0,1:T(8,128)(2,1)S(1)} %get-tuple-element.665, bf16[1024,1792]{0,1:T(8,128)(2,1)} %fusion.103, bf16[1024,1536]{0,1:T(8,128)(2,1)} %get-tuple-element.688), kind=kOutput, calls=%fused_computation.210 | convolution fusion | flops 5292834816 | bytes 18735104 | tf_op jit(solution)/shard_map/ti,tj->ij/dot_general | solution.py:199
  896.9 6.4 fusion.121
  903.3 4.1 copy.331
  907.9 11.7 reduce.22
  920.9 3.7 all-to-all-start.1
  924.6 10.7 fusion.114
  937.7 4.2 copy.330
  941.9 11.5 reduce.21
  954.8 20.8 %all-to-all-done.1 = bf16[16,2,24576]{2,1,0:T(2,128)(2,1)S(1)} async-done(((bf16[16,2,24576]{2,1,0:T(2,128)(2,1)}), bf16[16,2,24576]{2,1,0:T(2,128)(2,1)S(1)}, u32[]{:S(2)}, u32[]{:S(2)}) %all-to-all-start.1) | async-done | bytes 1572896 | tf_op jit(solution)/shard_map/all_to_all | solution.py:278
  975.5 27.4 %all-to-all-start.3 = ((bf16[16,2,24576]{2,1,0:T(2,128)(2,1)}), bf16[16,2,24576]{2,1,0:T(2,128)(2,1)S(1)}, u32[]{:S(2)}, u32[]{:S(2)}) async-start(bf16[16,2,24576]{2,1,0:T(2,128)(2,1)} %reshape.519), calls=%async_computation.3 | async-start | bytes 3145728 | tf_op jit(solution)/shard_map/all_to_all | solution.py:279
  1006.4 122.2 %reduce-scatter.6.cloned.1.call-done = f32[48,3352]{1,0:T(8,128)} async-done(((f32[768,3352]{1,0:T(8,128)}), f32[48,3352]{1,0:T(8,128)}) %reduce-scatter.6.cloned.1.call-update) | async-done | bytes 643600 | tf_op jit(solution)/shard_map/reduce_scatter | solution.py:296
  1128.9 75.2 %all-reduce.17 = (f32[768]{0:T(1024)S(1)}, f32[1792]{0:T(1024)S(1)}, f32[24]{0:T(128)S(1)}, f32[24]{0:T(128)S(1)}, f32[24]{0:T(128)S(1)}, /*index=5*/f32[1536]{0:T(1024)S(1)}) all-reduce(f32[768]{0:T(1024)S(1)} %get-tuple-element.592, f32[1792]{0:T(1024)S(1)} %get-tuple-element.590, ...), channel_id=2, replica_groups=mesh['rep'=2,'shard'=16] {'shard'}, use_global_device_ids=true, to_apply=%region_25.27.clone | all-reduce | flops 4168 | bytes 33344
  1204.3 3.9 reduce-scatter.10.cloned.1.call-done
  1212.1 6.3 reshape.518
  1220.5 6.3 reshape.520
  1233.9 3.4 broadcast_select_fusion
  (403 shorter events, 185.1 us)
Async XLA Ops:
  7.2 1.5 copy-start
  7.2 240.9 %all-gather.4.cloned.1.call-start = ((), (), s32[]{:S(2)}) async-start(), calls=%async_computation.7 | async-start | bytes 5640192 | tf_op jit(solution)/shard_map/all_gather | solution.py:250
  12.6 73.9 %copy-start.43 = (u32[32]{0:T(128)S(1)}, u32[32]{0:T(128)}, u32[]{:S(2)}) copy-start(u32[32]{0:T(128)} %constant.162) | copy-start | bytes 388
  12.6 76.5 %copy-start.46 = (bf16[112]{0:T(256)(128)(2,1)S(1)}, bf16[112]{0:T(256)(128)(2,1)}, u32[]{:S(2)}) copy-start(bf16[112]{0:T(256)(128)(2,1)} %param.26) | copy-start | bytes 676
  12.6 76.7 %copy-start.47 = (bf16[96]{0:T(256)(128)(2,1)S(1)}, bf16[96]{0:T(256)(128)(2,1)}, u32[]{:S(2)}) copy-start(bf16[96]{0:T(256)(128)(2,1)} %param.30) | copy-start | bytes 580
  12.6 77.0 %copy-start.48 = (bf16[48]{0:T(256)(128)(2,1)S(1)}, bf16[48]{0:T(256)(128)(2,1)}, u32[]{:S(2)}) copy-start(bf16[48]{0:T(256)(128)(2,1)} %param.23) | copy-start | bytes 292
  12.6 193.1 %copy-start.44 = (bf16[112,4]{0,1:T(4,128)(2,1)S(1)}, bf16[112,4]{0,1:T(4,128)(2,1)}, u32[]{:S(2)}) copy-start(bf16[112,4]{0,1:T(4,128)(2,1)} %param.25) | copy-start | bytes 2692
  12.6 228.9 %copy-start.45 = (f32[24]{0:T(128)S(1)}, f32[24]{0:T(128)}, u32[]{:S(2)}) copy-start(f32[24]{0:T(128)} %param.29) | copy-start | bytes 292
  12.7 229.0 %copy-start.49 = (s32[1,16]{1,0:T(1,128)S(1)}, s32[1,16]{1,0:T(1,128)}, u32[]{:S(2)}) copy-start(s32[1,16]{1,0:T(1,128)} %param.21) | copy-start | bytes 196
  12.7 230.4 %copy-start.51 = (f32[24]{0:T(128)S(1)}, f32[24]{0:T(128)}, u32[]{:S(2)}) copy-start(f32[24]{0:T(128)} %param.28) | copy-start | bytes 292
  81.1 178.3 %copy-start.5 = (bf16[16,1,64,768]{3,2,1,0:T(8,128)(2,1)}, bf16[16,1,64,768]{3,2,1,0:T(8,128)(2,1)S(1)}, u32[]{:S(2)}) copy-start(bf16[16,1,64,768]{3,2,1,0:T(8,128)(2,1)S(1)} %all_to_all.42) | copy-start | bytes 4718596
  81.1 164.1 %all-to-all-start.2 = ((bf16[16,1,64,768]{3,2,1,0:T(8,128)(2,1)}), bf16[16,1,64,768]{3,2,1,0:T(8,128)(2,1)}, u32[]{:S(2)}, u32[]{:S(2)}) async-start(bf16[16,1,64,768]{3,2,1,0:T(8,128)(2,1)} %get-tuple-element.700), calls=%async_computation.2 | async-start | bytes 3145728 | tf_op jit(solution)/shard_map/all_to_all | solution.py:244
  85.6 413.4 %all-gather.6.cloned.1.call-start = ((), (), s32[]{:S(2)}) async-start(), calls=%async_computation.8 | async-start | bytes 2506752 | tf_op jit(solution)/shard_map/all_gather | solution.py:254
  86.4 920.0 %reduce-scatter.8.cloned.1.call-start = ((), (), s32[]{:S(2)}) async-start(), calls=%async_computation.10 | async-start | bytes 5013504 | tf_op jit(solution)/shard_map/reduce_scatter | solution.py:300
  205.8 53.7 %copy-start.25 = (f32[768]{0:T(1024)}, f32[768]{0:T(1024)S(1)}, u32[]{:S(2)}) copy-start(f32[768]{0:T(1024)S(1)} %convert_element_type.160) | copy-start | bytes 9220
  241.7 265.1 %copy-start.31 = (f32[1536]{0:T(1024)}, f32[1536]{0:T(1024)S(1)}, u32[]{:S(2)}) copy-start(f32[1536]{0:T(1024)S(1)} %convert_element_type.165) | copy-start | bytes 18436
  242.9 16.5 %copy-start.34 = (f32[1024]{0:T(1024)}, f32[1024]{0:T(1024)S(1)}, u32[]{:S(2)}) copy-start(f32[1024]{0:T(1024)S(1)} %fusion.126) | copy-start | bytes 12292
  243.0 20.2 %copy-start.17 = (f32[1792]{0:T(1024)}, f32[1792]{0:T(1024)S(1)}, u32[]{:S(2)}) copy-start(f32[1792]{0:T(1024)S(1)} %get-tuple-element.594) | copy-start | bytes 21508
  243.1 20.2 %copy-start.19 = (f32[1792]{0:T(1024)}, f32[1792]{0:T(1024)S(1)}, u32[]{:S(2)}) copy-start(f32[1792]{0:T(1024)S(1)} %get-tuple-element.595) | copy-start | bytes 21508
  243.1 20.2 %copy-start.21 = (f32[1792]{0:T(1024)}, f32[1792]{0:T(1024)S(1)}, u32[]{:S(2)}) copy-start(f32[1792]{0:T(1024)S(1)} %get-tuple-element.596) | copy-start | bytes 21508
  243.1 20.2 %copy-start.23 = (f32[1792]{0:T(1024)}, f32[1792]{0:T(1024)S(1)}, u32[]{:S(2)}) copy-start(f32[1792]{0:T(1024)S(1)} %get-tuple-element.597) | copy-start | bytes 21508
  243.1 47.7 %copy-start.41 = (f32[24]{0:T(128)}, f32[24]{0:T(128)S(1)}, u32[]{:S(2)}) copy-start(f32[24]{0:T(128)S(1)} %exponential_negate_fusion) | copy-start | bytes 292
  243.6 15.9 %copy-start.29 = (f32[1024]{0:T(1024)}, f32[1024]{0:T(1024)S(1)}, u32[]{:S(2)}) copy-start(f32[1024]{0:T(1024)S(1)} %add.199) | copy-start | bytes 12292
  243.6 15.9 %copy-start.27 = (f32[1024]{0:T(1024)}, f32[1024]{0:T(1024)S(1)}, u32[]{:S(2)}) copy-start(f32[1024]{0:T(1024)S(1)} %rsqrt.20) | copy-start | bytes 12292
  263.3 10.1 copy-start.3
  273.4 2.9 copy-start.2
  278.4 12.4 copy-start.39
  291.9 0.6 copy-start.13
  483.5 8.3 copy-start.4
  483.6 10.9 copy-start.12
  491.9 2.6 copy-start.7
  491.9 14.9 %copy-start.36 = (f32[1024]{0:T(1024)}, f32[1024]{0:T(1024)S(1)}, u32[]{:S(2)}) copy-start(f32[1024]{0:T(1024)S(1)} %fusion.127) | copy-start | bytes 12292
  499.0 7.8 copy-start.8
  529.3 599.3 %reduce-scatter.6.cloned.1.call-start = ((), (), s32[]{:S(2)}) async-start(), calls=%async_computation.9 | async-start | bytes 11280384 | tf_op jit(solution)/shard_map/reduce_scatter | solution.py:296
  828.8 7.1 copy-start.9
  828.8 7.3 copy-start.10
  828.8 7.5 copy-start.15
  828.8 7.5 copy-start.16
  828.8 7.6 copy-start.14
  828.8 7.6 copy-start.40
  828.8 7.6 copy-start.42
  842.8 19.0 %copy-start.18 = (f32[1792]{0:T(1024)S(1)}, f32[1792]{0:T(1024)}, u32[]{:S(2)}) copy-start(f32[1792]{0:T(1024)} %copy-done.17) | copy-start | bytes 21508
  842.8 19.0 %copy-start.20 = (f32[1792]{0:T(1024)S(1)}, f32[1792]{0:T(1024)}, u32[]{:S(2)}) copy-start(f32[1792]{0:T(1024)} %copy-done.19) | copy-start | bytes 21508
  842.8 19.0 %copy-start.22 = (f32[1792]{0:T(1024)S(1)}, f32[1792]{0:T(1024)}, u32[]{:S(2)}) copy-start(f32[1792]{0:T(1024)} %copy-done.21) | copy-start | bytes 21508
  842.8 19.0 %copy-start.24 = (f32[1792]{0:T(1024)S(1)}, f32[1792]{0:T(1024)}, u32[]{:S(2)}) copy-start(f32[1792]{0:T(1024)} %copy-done.23) | copy-start | bytes 21508
  870.4 12.1 copy-start.11
  895.4 1.4 copy-start.6
  895.4 1.4 copy-start.32
  895.4 1.4 copy-start.35
  895.4 1.4 copy-start.37
  907.4 17.2 %copy-start.26 = (f32[768]{0:T(1024)S(1)}, f32[768]{0:T(1024)}, u32[]{:S(2)}) copy-start(f32[768]{0:T(1024)} %copy-done.25) | copy-start | bytes 9220
  907.4 17.2 %copy-start.28 = (f32[1024]{0:T(1024)S(1)}, f32[1024]{0:T(1024)}, u32[]{:S(2)}) copy-start(f32[1024]{0:T(1024)} %copy-done.27) | copy-start | bytes 12292
  920.9 54.6 %all-to-all-start.1 = ((bf16[16,2,24576]{2,1,0:T(2,128)(2,1)}), bf16[16,2,24576]{2,1,0:T(2,128)(2,1)S(1)}, u32[]{:S(2)}, u32[]{:S(2)}) async-start(bf16[16,2,24576]{2,1,0:T(2,128)(2,1)} %reshape.517), calls=%async_computation.1 | async-start | bytes 3145728 | tf_op jit(solution)/shard_map/all_to_all | solution.py:278
  924.6 10.7 copy-start.30
  941.9 62.5 %copy-start.50 = (s32[1,16]{1,0:T(1,128)S(1)}, s32[1,16]{1,0:T(1,128)}, u32[]{:S(2)}) copy-start(s32[1,16]{1,0:T(1,128)} %param.22) | copy-start | bytes 196
  941.9 186.7 %copy-start.33 = (f32[1536]{0:T(1024)S(1)}, f32[1536]{0:T(1024)}, u32[]{:S(2)}) copy-start(f32[1536]{0:T(1024)} %get-tuple-element.662) | copy-start | bytes 18436
  941.9 186.9 %copy-start.52 = (f32[24]{0:T(128)S(1)}, f32[24]{0:T(128)}, u32[]{:S(2)}) copy-start(f32[24]{0:T(128)} %param.28) | copy-start | bytes 292
  941.9 187.0 %copy-start.38 = (f32[1536]{0:T(1024)S(1)}, f32[1536]{0:T(1024)}, u32[]{:S(2)}) copy-start(f32[1536]{0:T(1024)} %get-tuple-element.588) | copy-start | bytes 18436
  975.5 245.0 %all-to-all-start.3 = ((bf16[16,2,24576]{2,1,0:T(2,128)(2,1)}), bf16[16,2,24576]{2,1,0:T(2,128)(2,1)S(1)}, u32[]{:S(2)}, u32[]{:S(2)}) async-start(bf16[16,2,24576]{2,1,0:T(2,128)(2,1)} %reshape.519), calls=%async_computation.3 | async-start | bytes 3145728 | tf_op jit(solution)/shard_map/all_to_all | solution.py:279
  1002.9 205.3 %reduce-scatter.10.cloned.1.call-start = ((), (), s32[]{:S(2)}) async-start(), calls=%async_computation.11 | async-start | bytes 974848
  1004.3 233.0 %all-reduce.23.cloned.1.call-start = ((), (), s32[]{:S(2)}) async-start(), calls=%async_computation.12 | async-start | bytes 1916928 | tf_op jit(solution)/shard_map/psum | solution.py:283
  1230.1 10.9 copy-start.1
Sparse Core Ops, SparseCore 0:
  10.8 132.4 all-gather.3
  146.1 62.0 all-gather.5
  529.4 135.1 reduce-scatter.7
  895.6 232.9 reduce-scatter.5
  1131.3 76.8 reduce-scatter.9
  1210.6 15.8 all-reduce.22
